TPU v7x, 256 devices: a whole 4x4x8 slice. The times are simulated.
256 devices in a mesh: dp: 4 (over x), expert: 64 (over z, y, core).
Axes of the slice: x: 4, y: 4, z: 8, core: 2. Of those that a mesh axis runs over, the one named last changes fastest.
Arguments:
- tokens: bfloat16 [4096, 3584], P('expert'), may hold values from -6 to 6
- expert_ids: int32 [4096, 8], P('expert'), may hold values from 0 to 63, all different within a row; in each aligned block of 64 rows (0 to 63, 64 to 127, ...) at most 8 rows name the same one
- weight_num: int32 [4096, 8], P('expert'), may hold values from 64 to 1023
- gate_proj: bfloat16 [64, 3584, 2048], P('expert', None, 'dp'), may hold values from -0.09375 to 0.09375
- up_proj: bfloat16 [64, 3584, 2048], P('expert', None, 'dp'), may hold values from -0.09375 to 0.09375
- down_proj: bfloat16 [64, 2048, 3584], P('expert', 'dp'), may hold values from -0.125 to 0.125
Outputs:
- combined: bfloat16 [4096, 3584], P('expert', 'dp')
Inputs may be any that keep to these rules, and one draw needn't show every extreme that they name: `expert_ids`: in the 64 rows of one device no expert is named by more than 8 rows, and some device has an expert named by exactly 8 of its rows.
All inputs are finite; a program needn't handle non-finite values.
Results may differ from a plain program's by a relative error of at most 0.015.
Values may be sent and summed in bfloat16 or wider, within the bound.
A program may use at most 192 MiB of HBM per device.

v0:
```python
import jax
import jax.numpy as jnp
from jax import lax
from jax.sharding import PartitionSpec as P

ROOM = 8


def routing_table(block_ids, expert_total, capacity):
    row_count = block_ids.shape[0]
    top_count = block_ids.shape[1]
    flat_ids = block_ids.reshape(-1)
    onehot = (flat_ids[:, None] == jnp.arange(expert_total, dtype=jnp.int32)[None, :]).astype(
        jnp.int32
    )
    before = jnp.cumsum(onehot, axis=0) - onehot
    position = jnp.sum(before * onehot, axis=1)
    target = flat_ids * capacity + position
    owners = jnp.full((expert_total * capacity,), row_count * top_count, jnp.int32)
    owners = owners.at[target].set(jnp.arange(row_count * top_count, dtype=jnp.int32))
    return (target, owners)


def local(tokens, expert_ids, weight_num, gate_proj, up_proj, down_proj):
    experts = lax.axis_size("expert")
    row_count, top_count = expert_ids.shape
    feature_width = tokens.shape[1]
    capacity = max(ROOM, (row_count * top_count + experts - 1) // experts)
    target, owners = routing_table(expert_ids, experts, capacity)
    usable = owners < row_count * top_count
    source_row = jnp.where(usable, owners // top_count, 0)
    outgoing = jnp.where(usable[:, None], tokens[source_row], jnp.zeros((), tokens.dtype))
    outgoing = outgoing.reshape(experts, capacity, feature_width)
    gate_share = gate_proj[0]
    up_share = up_proj[0]
    down_share = down_proj[0]
    block_rows = lax.all_to_all(outgoing, "expert", split_axis=0, concat_axis=0, tiled=True)
    flat_rows = block_rows.reshape(-1, feature_width)
    gate_out = jnp.dot(flat_rows, gate_share, preferred_element_type=jnp.float32)
    up_out = jnp.dot(flat_rows, up_share, preferred_element_type=jnp.float32)
    hidden = (jax.nn.silu(gate_out) * up_out).astype(jnp.bfloat16)
    share_out = jnp.dot(hidden, down_share, preferred_element_type=jnp.float32).astype(jnp.bfloat16)
    partial_value = share_out.reshape(block_rows.shape[0], block_rows.shape[1], feature_width)
    weights = weight_num.astype(jnp.float32) / 1024.0
    summed = lax.psum_scatter(partial_value, "dp", scatter_dimension=2, tiled=True).astype(
        jnp.float32
    )
    returned = lax.all_to_all(
        summed.astype(jnp.bfloat16), "expert", split_axis=0, concat_axis=0, tiled=True
    ).astype(summed.dtype)
    quarter_width = returned.shape[2]
    picked = returned.reshape(experts * capacity, quarter_width)[target].reshape(
        row_count, top_count, quarter_width
    )
    combined = jnp.sum(picked * weights[:, :, None], axis=1)
    return combined.astype(jnp.bfloat16)


def solution(mesh):
    placed = (
        P("expert", None),
        P("expert", None),
        P("expert", None),
        P("expert", None, "dp"),
        P("expert", None, "dp"),
        P("expert", "dp", None),
    )
    return jax.shard_map(
        local, mesh=mesh, in_specs=placed, out_specs=P("expert", "dp"), check_vma=False
    )
```

profile of v0, /device:TPU:1, one launch (start us, length us, event | category | flops | bytes accessed | tf_op | source)
XLA Modules:
  0.0 388.6 jit_solution(145485025298980232)
XLA Ops:
  6.5 0.8 copy.14
  7.5 0.7 broadcast_multiply_fusion
  8.3 1.2 reduce-window.6
  9.5 0.2 slice_reduce_fusion
  9.8 0.1 mul.36
  9.9 0.1 fusion.26
  10.1 2.4 scatter_custom_fusion
  12.6 0.1 broadcast_in_dim.24
  12.7 4.2 %gather_fusion = bf16[512,3584]{1,0:T(8,128)(2,1)} fusion(bf16[64,3584]{1,0:T(8,128)(2,1)S(1)} %copy-done, s32[1024]{0:T(1024)S(1)} %pad_clamp_fusion.1), kind=kCustom, calls=%fused_computation | custom fusion | bytes 7342080 | tf_op jit(solution)/shard_map/gather | solution.py:32
  16.8 2.3 bitcast_select_fusion
  19.2 97.2 %all_to_all.10 = bf16[64,8,3584]{2,1,0:T(8,128)(2,1)S(1)} all-to-all(bf16[64,8,3584]{2,1,0:T(8,128)(2,1)S(1)} %bitcast_select_fusion), channel_id=1, replica_groups=mesh['dp'=4,'expert'=64] {'expert'}, dimensions={0} | all-to-all | bytes 7340032 | tf_op jit(solution)/shard_map/all_to_all | solution.py:37
  116.4 1.8 copy-done.2
  118.2 2.0 fusion.4
  120.3 10.0 %fusion = bf16[64,8,3584]{2,1,0:T(8,128)(2,1)} fusion(bf16[1,512,3584]{2,1,0:T(8,128)(2,1)} %param.11, bf16[1,3584,512]{2,1,0:T(8,128)(2,1)} %param.10, bf16[64,8,3584]{2,1,0:T(8,128)(2,1)} %copy-done.2, f32[512,512]{1,0:T(8,128)S(1)} %fusion.4), kind=kOutput, calls=%fused_computation.4 | convolution fusion | flops 3761504256 | bytes 15728640 | tf_op jit(solution)/shard_map/dot_general | solution.py:42
  130.3 47.2 %copy.18 = bf16[64,8,3584]{1,0,2:T(8,128)(2,1)} copy(bf16[64,8,3584]{2,1,0:T(8,128)(2,1)} %fusion) | data formatting | bytes 7340032
  177.6 83.6 %reshape.103 = bf16[3584,512]{1,0:T(8,128)(2,1)} reshape(bf16[3584,64,8]{2,1,0:T(8,128)(2,1)} %bitcast.60) | data formatting | bytes 7340032
  261.2 42.3 %reduce-scatter.4.cloned.1.call-done = bf16[896,512]{1,0:T(8,128)(2,1)} async-done(((bf16[3584,512]{1,0:T(8,128)(2,1)}), bf16[896,512]{1,0:T(8,128)(2,1)}) %reduce-scatter.4.cloned.1.call-update) | async-done | bytes 917520
  303.5 19.4 %reshape.104 = bf16[896,64,8]{2,1,0:T(8,128)(2,1)} reshape(bf16[896,512]{1,0:T(8,128)(2,1)} %reduce-scatter.4.cloned.1.call-done) | data formatting | bytes 1835008
  322.8 17.5 %copy.19 = bf16[64,8,896]{2,1,0:T(8,128)(2,1)} copy(bf16[64,8,896]{1,0,2:T(8,128)(2,1)} %bitcast.61) | data formatting | bytes 1835008
  340.3 10.6 %all-to-all-start.1 = ((bf16[64,8,896]{2,1,0:T(8,128)(2,1)}), bf16[64,8,896]{2,1,0:T(8,128)(2,1)S(1)}, u32[]{:S(2)}, u32[]{:S(2)}) async-start(bf16[64,8,896]{2,1,0:T(8,128)(2,1)} %copy.19), calls=%async_computation.1 | async-start | bytes 1835008 | tf_op jit(solution)/shard_map/all_to_all | solution.py:48
  351.1 25.2 %all-to-all-done.1 = bf16[64,8,896]{2,1,0:T(8,128)(2,1)S(1)} async-done(((bf16[64,8,896]{2,1,0:T(8,128)(2,1)}), bf16[64,8,896]{2,1,0:T(8,128)(2,1)S(1)}, u32[]{:S(2)}, u32[]{:S(2)}) %all-to-all-start.1) | async-done | bytes 917536 | tf_op jit(solution)/shard_map/all_to_all | solution.py:48
  376.2 0.1 bitcast_convert_fusion
  376.4 2.7 gather_fusion.1
  379.1 2.7 fusion.8
  (25 shorter events, 0.5 us)
Async XLA Ops:
  6.5 6.1 %copy-start = (bf16[64,3584]{1,0:T(8,128)(2,1)S(1)}, bf16[64,3584]{1,0:T(8,128)(2,1)}, u32[]{:S(2)}) copy-start(bf16[64,3584]{1,0:T(8,128)(2,1)} %param.6) | copy-start | bytes 1376260
  6.5 296.9 %reduce-scatter.4.cloned.1.call-start = ((), (), s32[]{:S(2)}) async-start(), calls=%async_computation.3 | async-start | bytes 4587520
  19.2 99.1 %copy-start.4 = (bf16[1,3584,512]{2,1,0:T(8,128)(2,1)S(1)}, bf16[1,3584,512]{2,1,0:T(8,128)(2,1)}, u32[]{:S(2)}) copy-start(bf16[1,3584,512]{2,1,0:T(8,128)(2,1)} %param.9) | copy-start | bytes 11010052
  116.4 1.8 copy-start.2
  322.8 28.1 %copy-start.3 = (s32[64,8]{0,1:T(8,128)S(1)}, s32[64,8]{0,1:T(8,128)}, u32[]{:S(2)}) copy-start(s32[64,8]{0,1:T(8,128)} %param.8) | copy-start | bytes 6148
  340.3 35.9 %all-to-all-start.1 = ((bf16[64,8,896]{2,1,0:T(8,128)(2,1)}), bf16[64,8,896]{2,1,0:T(8,128)(2,1)S(1)}, u32[]{:S(2)}, u32[]{:S(2)}) async-start(bf16[64,8,896]{2,1,0:T(8,128)(2,1)} %copy.19), calls=%async_computation.1 | async-start | bytes 1835008 | tf_op jit(solution)/shard_map/all_to_all | solution.py:48
  376.4 5.4 %copy-start.1 = (bf16[64,3584]{1,0:T(8,128)(2,1)S(1)}, bf16[64,3584]{1,0:T(8,128)(2,1)}, u32[]{:S(2)}) copy-start(bf16[64,3584]{1,0:T(8,128)(2,1)} %param.6) | copy-start | bytes 1376260
Sparse Core Ops, SparseCore 0:
  261.3 42.1 reduce-scatter.3
where the time goes:
time: 391 us; the launch traced here: 389 us
  local copies, waits for them, and re-layouts  180 us (46%)
  blocking collectives  97.2 us (25%)
  waiting for transfers between devices  67.5 us (17%)
  between operations  13.5 us (3%)
  matrix products  12.1 us (3%)
  starting transfers between devices  10.6 us (3%)
  other arithmetic  7.28 us (2%)
    unnamed x15, local copies, waits for them, and re-layouts  170 us
    all_to_all x1, blocking collectives, local(): lax.all_to_all(outgoing, 'expert', split_axis=0, concat_axis=0, tiled=True)  97.2 us
    unnamed x2, waiting for transfers between devices  42.3 us
    all_to_all x1, waiting for transfers between devices, local(): lax.all_to_all(summed.astype(jnp.bfloat16), 'expert', split_axis=0, conca...  25.2 us
    all_to_all x1, starting transfers between devices, local(): lax.all_to_all(summed.astype(jnp.bfloat16), 'expert', split_axis=0, conca...  10.6 us
    dot_general x1, matrix products, local(): jnp.dot(hidden, down_share, preferred_element_type=jnp.float32)  10 us
  transfers between devices with their start and end apart: 2, of which 2 were waited for; matrix products, arithmetic and copies ran while one was open for 0% of the time, Pallas kernels for 0%

commit v1 on v0

v1 whole, which is shorter than its diff:
```python
import jax
import jax.numpy as jnp
from jax import lax
from jax.sharding import PartitionSpec as P

ROOM = 8


def slot_matrices(ids, num, experts, capacity):
    rows = ids.shape[0]
    slots = experts * capacity
    column = jnp.arange(slots, dtype=jnp.int32)[None, :]
    expert_of = column // capacity
    hits = [ids[:, k : k + 1] == expert_of for k in range(ids.shape[1])]
    named = sum(h.astype(jnp.float32) for h in hits)
    weight = sum(jnp.where(h, num[:, k : k + 1], 0) for k, h in enumerate(hits))
    earlier = jnp.arange(rows)[:, None] > jnp.arange(rows)[None, :]
    position = jnp.dot(
        earlier.astype(jnp.bfloat16), named.astype(jnp.bfloat16), preferred_element_type=jnp.float32
    )
    here = (named > 0) & (position == (column % capacity).astype(jnp.float32))
    high = jnp.where(here, weight // 32 * 32, 0).astype(jnp.bfloat16)
    low = jnp.where(here, weight % 32, 0).astype(jnp.bfloat16)
    return here.astype(jnp.bfloat16), high, low


def local(tokens, expert_ids, weight_num, gate_proj, up_proj, down_proj):
    experts = lax.axis_size("expert")
    parts = lax.axis_size("dp")
    width = tokens.shape[1]
    quarter = width // parts
    slots = experts * ROOM
    here, high, low = slot_matrices(expert_ids, weight_num, experts, ROOM)
    mine = lax.dynamic_slice_in_dim(tokens, lax.axis_index("dp") * quarter, quarter, 1)
    outgoing = lax.dot_general(
        here, mine, (((0,), (0,)), ((), ())), preferred_element_type=jnp.float32
    ).astype(jnp.bfloat16)
    arrived = lax.all_to_all(
        outgoing.reshape(experts, ROOM, quarter), "expert", split_axis=0, concat_axis=0, tiled=True
    ).reshape(slots, quarter)
    rows = lax.all_gather(arrived, "dp", axis=0, tiled=True)
    gate_out, up_out = 0.0, 0.0
    for q in range(parts):
        block = rows[q * slots : (q + 1) * slots]
        cut = slice(q * quarter, (q + 1) * quarter)
        gate_out += jnp.dot(block, gate_proj[0, cut], preferred_element_type=jnp.float32)
        up_out += jnp.dot(block, up_proj[0, cut], preferred_element_type=jnp.float32)
    hidden = (jax.nn.silu(gate_out) * up_out).astype(jnp.bfloat16)
    partial = jnp.concatenate(
        [
            jnp.dot(
                hidden,
                down_proj[0, :, q * quarter : (q + 1) * quarter],
                preferred_element_type=jnp.float32,
            ).astype(jnp.bfloat16)
            for q in range(parts)
        ],
        axis=0,
    )
    summed = lax.psum_scatter(partial, "dp", scatter_dimension=0, tiled=True)
    returned = lax.all_to_all(
        summed.reshape(experts, ROOM, quarter), "expert", split_axis=0, concat_axis=0, tiled=True
    ).reshape(slots, quarter)
    total = jnp.dot(high, returned, preferred_element_type=jnp.float32)
    total += jnp.dot(low, returned, preferred_element_type=jnp.float32)
    return (total / 1024.0).astype(jnp.bfloat16)


def solution(mesh):
    placed = (
        P("expert", None),
        P("expert", None),
        P("expert", None),
        P("expert", None, "dp"),
        P("expert", None, "dp"),
        P("expert", "dp", None),
    )
    return jax.shard_map(
        local, mesh=mesh, in_specs=placed, out_specs=P("expert", "dp"), check_vma=False
    )
```

time: 391 us -> 203 us (0.52)
  local copies, waits for them, and re-layouts: 180 us -> 2.81 us
  blocking collectives: 97.2 us -> 38.4 us
  waiting for transfers between devices: 67.5 us -> 115 us
    unnamed x15 -> x12, local copies, waits for them, and re-layouts: 170 us -> 1.82 us
    all_to_all x1, blocking collectives: 97.2 us -> 38.4 us  [local(): lax.all_to_all(outgoing.reshape(experts, ROOM, quarter), 'expert', split_...]
    reduce_scatter x0 -> x1, waiting for transfers between devices: none -> 45.6 us  [local(): summed = lax.psum_scatter(partial, 'dp', scatter_dimension=0, tiled=True)]
    all_gather x0 -> x1, waiting for transfers between devices: none -> 43.6 us  [local(): rows = lax.all_gather(arrived, 'dp', axis=0, tiled=True)]
    unnamed x2, waiting for transfers between devices: 42.3 us -> 0.03 us
    concatenate x0 -> x1, other arithmetic: none -> 8.72 us  [local(): jnp.concatenate([jnp.dot(hidden, down_proj[0, :, q * quarter:(q + 1) * qu...]
    gather x2 -> x0, local copies, waits for them, and re-layouts: 6.85 us -> none  [the longest x1 4.16 us: local(): tokens[source_row]]
    dot_general x2 -> x16, matrix products: 12.1 us -> 14.4 us  [the longest x4 6.26 us: local(): jnp.dot(block, gate_proj[0, cut], preferred_element_type=jnp.float32)]
  transfers between devices with their start and end apart: 2 -> 3, of which waited for: 2 -> 3; matrix products, arithmetic and copies ran while one was open for 0% -> 0% of each run, Pallas kernels for 0% -> 0%
where the time goes in v1:
time: 203 us
  waiting for transfers between devices  115 us (57%)
  blocking collectives  38.4 us (19%)
  matrix products  14.4 us (7%)
  between operations  13.6 us (7%)
  starting transfers between devices  10.7 us (5%)
  other arithmetic  8.73 us (4%)
  local copies, waits for them, and re-layouts  2.81 us (1%)
    reduce_scatter x1, waiting for transfers between devices, local(): summed = lax.psum_scatter(partial, 'dp', scatter_dimension=0, tiled=True)  45.6 us
    all_gather x1, waiting for transfers between devices, local(): rows = lax.all_gather(arrived, 'dp', axis=0, tiled=True)  43.6 us
    all_to_all x1, blocking collectives, local(): lax.all_to_all(outgoing.reshape(experts, ROOM, quarter), 'expert', split_...  38.4 us
    all_to_all x1, waiting for transfers between devices, local(): lax.all_to_all(summed.reshape(experts, ROOM, quarter), 'expert', split_ax...  25.3 us
    all_to_all x1, starting transfers between devices, local(): lax.all_to_all(summed.reshape(experts, ROOM, quarter), 'expert', split_ax...  10.6 us
    concatenate x1, other arithmetic, local(): jnp.concatenate([jnp.dot(hidden, down_proj[0, :, q * quarter:(q + 1) * qu...  8.72 us
    dot_general x4, matrix products, local(): jnp.dot(block, gate_proj[0, cut], preferred_element_type=jnp.float32)  6.26 us
  transfers between devices with their start and end apart: 3, of which 3 were waited for; matrix products, arithmetic and copies ran while one was open for 0% of the time, Pallas kernels for 0%

profile of v1, /device:TPU:1, one launch (start us, length us, event | category | flops | bytes accessed | tf_op | source)
XLA Modules:
  0.0 203.0 jit_solution(10615380470221626891)
XLA Ops:
  6.5 1.0 slice_bitcast_fusion.15
  7.9 0.5 fusion.1
  8.3 38.4 %all_to_all.10 = bf16[64,8,896]{2,1,0:T(8,128)(2,1)} all-to-all(bf16[64,8,896]{2,1,0:T(8,128)(2,1)S(1)} %fusion.1), channel_id=1, replica_groups=mesh['dp'=4,'expert'=64] {'expert'}, dimensions={0} | all-to-all | bytes 1835008 | tf_op jit(solution)/shard_map/all_to_all | solution.py:38
  46.8 43.6 %all-gather.2.cloned.1.call-done = bf16[2048,896]{1,0:T(8,128)(2,1)} async-done(((bf16[512,896]{1,0:T(8,128)(2,1)}), bf16[2048,896]{1,0:T(8,128)(2,1)}) %all-gather.2.cloned.1.call-update) | async-done | bytes 3670032 | tf_op jit(solution)/shard_map/all_gather | solution.py:41
  90.4 2.3 %fusion.21 = f32[512,512]{1,0:T(8,128)S(1)} fusion(bf16[1,3584,512]{2,1,0:T(8,128)(2,1)} %param.9, bf16[2048,896]{1,0:T(8,128)(2,1)} %all-gather.2.cloned.1.call-done), kind=kOutput, calls=%fused_computation.35 | convolution fusion | flops 469762048 | bytes 2883584 | tf_op jit(solution)/shard_map/dot_general | solution.py:46
  92.7 2.5 %convolution_add_fusion.5 = f32[512,512]{1,0:T(8,128)S(1)} fusion(f32[512,512]{1,0:T(8,128)S(1)} %fusion.21, bf16[1,3584,512]{2,1,0:T(8,128)(2,1)} %param.9, bf16[2048,896]{1,0:T(8,128)(2,1)} %all-gather.2.cloned.1.call-done), kind=kOutput, calls=%fused_computation.12 | convolution fusion | flops 470024192 | bytes 3932160 | tf_op jit(solution)/shard_map/dot_general | solution.py:46
  95.3 0.7 convolution_add_fusion.4
  96.0 0.7 convolution_add_fusion.3
  96.7 0.6 copy-done.3
  97.3 0.7 fusion.16
  98.0 0.7 convolution_add_fusion.2
  98.7 0.7 convolution_add_fusion.1
  99.5 0.8 fusion.2
  100.3 1.2 copy-done.5
  101.5 0.7 convolution_convert_fusion.1
  102.2 0.7 convolution_convert_fusion.2
  102.9 0.7 convolution_convert_fusion.3
  103.7 0.7 convolution_convert_fusion.4
  104.4 8.7 %pad_maximum_fusion = bf16[2048,896]{1,0:T(8,128)(2,1)} fusion(bf16[512,896]{1,0:T(8,128)(2,1)S(1)} %convolution_convert_fusion.1, bf16[512,896]{1,0:T(8,128)(2,1)S(1)} %convolution_convert_fusion.2, bf16[512,896]{1,0:T(8,128)(2,1)S(1)} %convolution_convert_fusion.3, bf16[512,896]{1,0:T(8,128)(2,1)S(1)} %convolution_convert_fusion.4), kind=kLoop, calls=%fused_computation | loop fusion | flops 14680064 | bytes 7340032 | tf_op jit(solution)/shard_map/concatenate | solution.py:49
  113.1 45.6 %reduce-scatter.2.cloned.1.call-done = bf16[512,896]{1,0:T(8,128)(2,1)} async-done(((bf16[2048,896]{1,0:T(8,128)(2,1)}), bf16[512,896]{1,0:T(8,128)(2,1)}) %reduce-scatter.2.cloned.1.call-update) | async-done | bytes 917520 | tf_op jit(solution)/shard_map/reduce_scatter | solution.py:60
  158.7 10.6 %all-to-all-start.1 = ((bf16[64,8,896]{2,1,0:T(8,128)(2,1)}), bf16[64,8,896]{2,1,0:T(8,128)(2,1)S(1)}, u32[]{:S(2)}, u32[]{:S(2)}) async-start(bf16[64,8,896]{2,1,0:T(8,128)(2,1)} %bitcast.83), calls=%async_computation.2 | async-start | bytes 1835008 | tf_op jit(solution)/shard_map/all_to_all | solution.py:61
  169.4 25.3 %all-to-all-done.1 = bf16[64,8,896]{2,1,0:T(8,128)(2,1)S(1)} async-done(((bf16[64,8,896]{2,1,0:T(8,128)(2,1)}), bf16[64,8,896]{2,1,0:T(8,128)(2,1)S(1)}, u32[]{:S(2)}, u32[]{:S(2)}) %all-to-all-start.1) | async-done | bytes 917536 | tf_op jit(solution)/shard_map/all_to_all | solution.py:61
  194.6 0.5 fusion.7
  195.1 1.1 fusion.4
  (17 shorter events, 0.4 us)
Async XLA Ops:
  6.5 1.3 copy-start
  6.5 83.9 %all-gather.2.cloned.1.call-start = ((), (), s32[]{:S(2)}) async-start(), calls=%async_computation.3 | async-start | bytes 4587520 | tf_op jit(solution)/shard_map/all_gather | solution.py:41
  46.7 112.0 %reduce-scatter.2.cloned.1.call-start = ((), (), s32[]{:S(2)}) async-start(), calls=%async_computation.4 | async-start | bytes 4587520 | tf_op jit(solution)/shard_map/reduce_scatter | solution.py:60
  90.4 4.9 %copy-start.1 = (bf16[2048,896]{1,0:T(8,128)(2,1)S(1)}, bf16[2048,896]{1,0:T(8,128)(2,1)}, u32[]{:S(2)}) copy-start(bf16[2048,896]{1,0:T(8,128)(2,1)} %all-gather.2.cloned.1.call-done) | copy-start | bytes 11010052
  90.4 4.9 %copy-start.2 = (bf16[1,3584,512]{2,1,0:T(8,128)(2,1)S(1)}, bf16[1,3584,512]{2,1,0:T(8,128)(2,1)}, u32[]{:S(2)}) copy-start(bf16[1,3584,512]{2,1,0:T(8,128)(2,1)} %param.9) | copy-start | bytes 11010052
  95.3 2.0 %copy-start.3 = (bf16[1,3584,512]{2,1,0:T(8,128)(2,1)S(1)}, bf16[1,3584,512]{2,1,0:T(8,128)(2,1)}, u32[]{:S(2)}) copy-start(bf16[1,3584,512]{2,1,0:T(8,128)(2,1)} %param.10) | copy-start | bytes 11010052
  99.5 2.0 %copy-start.5 = (bf16[1,512,3584]{2,1,0:T(8,128)(2,1)S(1)}, bf16[1,512,3584]{2,1,0:T(8,128)(2,1)}, u32[]{:S(2)}) copy-start(bf16[1,512,3584]{2,1,0:T(8,128)(2,1)} %param.11) | copy-start | bytes 11010052
  113.1 56.2 %copy-start.4 = (s32[64,8]{0,1:T(8,128)S(1)}, s32[64,8]{0,1:T(8,128)}, u32[]{:S(2)}) copy-start(s32[64,8]{0,1:T(8,128)} %param.8) | copy-start | bytes 6148
  158.7 35.9 %all-to-all-start.1 = ((bf16[64,8,896]{2,1,0:T(8,128)(2,1)}), bf16[64,8,896]{2,1,0:T(8,128)(2,1)S(1)}, u32[]{:S(2)}, u32[]{:S(2)}) async-start(bf16[64,8,896]{2,1,0:T(8,128)(2,1)} %bitcast.83), calls=%async_computation.2 | async-start | bytes 1835008 | tf_op jit(solution)/shard_map/all_to_all | solution.py:61
Sparse Core Ops, SparseCore 0:
  46.8 43.5 all-gather.1
  113.2 45.3 reduce-scatter.1
